TPU v7x, 256 devices: a whole 4x4x8 slice. The times are simulated.
256 devices in a mesh: row: 32 (over x, z), col: 8 (over y, core).
Axes of the slice: x: 4, y: 4, z: 8, core: 2. Of those that a mesh axis runs over, the one named last changes fastest.
Arguments:
- matrix: float32 [2, 32, 256, 8, 8, 256], P(None, 'row', None, None, 'col'), may hold values from -160 to 8000, as said below
Outputs:
- trailing: float32 [2, 32, 256, 8, 8, 256], P(None, 'row', None, None, 'col')
- factor_panels: float32 [2, 32, 256, 768], P(None, 'row')
Inputs may be any that keep to these rules, and one draw needn't show every extreme that they name: matrix is symmetric positive definite with condition number at most about 2,000.
All inputs are finite; a program needn't handle non-finite values.
Results may differ from a plain program's by a relative error of at most 0.00018.
Values sent between devices are 32-bit elements; how exact they have to be, the bound alone decides.
A program may use at most 64 MiB of HBM per device.

v0:
```python
import jax
import jax.numpy as jnp
from jax import lax
from jax.sharding import PartitionSpec as P

PANELS = 3


def from_root(shard, axis, root):
    mine = lax.axis_index(axis) == root
    return lax.psum(jnp.where(mine, shard, jnp.zeros_like(shard)), axis)


def body(matrix):
    rows_count = lax.axis_size("row")
    cols_count = lax.axis_size("col")
    ratio = rows_count // cols_count
    my_row = lax.axis_index("row")
    my_col = lax.axis_index("col")
    tile_rows = matrix.shape[0]
    tile = matrix.shape[2]
    tile_cols = matrix.shape[3]
    work = matrix.reshape(tile_rows, tile, tile_cols, tile)
    row_tiles = jnp.arange(tile_rows) * rows_count + my_row
    highest = lax.Precision.HIGHEST
    collected = []
    for step in range(PANELS):
        first_row = step // rows_count
        first_col = step // cols_count
        corner = from_root(work[first_row, :, first_col, :], "row", step % rows_count)
        lower = jnp.linalg.cholesky(corner)
        inverse = jax.scipy.linalg.solve_triangular(
            lower, jnp.eye(tile, dtype=jnp.float32), lower=True
        )
        column = work[:, :, first_col, :]
        panel = jnp.einsum("aik,jk->aij", column, inverse, precision=highest)
        panel = jnp.where((row_tiles >= step)[:, None, None], panel, jnp.zeros_like(panel))
        panel = from_root(panel, "col", step % cols_count)
        received = []
        for turn in range(ratio):
            received.append(from_root(panel, "row", my_col + turn * cols_count))
        mirrored = jnp.stack(received, axis=1).reshape(tile_cols, tile, tile)
        work = work - jnp.einsum("aik,cjk->aicj", panel, mirrored, precision=highest)
        collected.append(panel)
    trailing = work.reshape(matrix.shape)
    factor_panels = jnp.concatenate(collected, axis=2).reshape(tile_rows, 1, tile, PANELS * tile)
    return (trailing, factor_panels)


def solution(mesh):
    in_specs = (P(None, "row", None, None, "col", None),)
    out_specs = (P(None, "row", None, None, "col", None), P(None, "row", None, None))
    return jax.shard_map(body, mesh=mesh, in_specs=in_specs, out_specs=out_specs, check_vma=False)
```

profile of v0, /device:TPU:18, one launch (start us, length us, event | category | flops | bytes accessed | tf_op | source)
XLA Modules:
  0.0 1370.9 jit_solution(15634683241599408947)
XLA Ops:
  7.2 10.9 copy.20
  19.9 147.2 %all-reduce.14.cloned.1.call-done = f32[256,256]{0,1:T(8,128)} async-done(((f32[256,256]{0,1:T(8,128)}), f32[256,256]{0,1:T(8,128)}) %all-reduce.14.cloned.1.call-update) | async-done | bytes 262160 | tf_op jit(solution)/shard_map/psum | solution.py:11
  169.2 11.7 cholesky.172
  181.0 9.8 custom-call.15
  191.3 11.7 cholesky.189
  205.2 4.6 while.6
  209.9 19.7 %custom-call.16 = f32[2,128,128]{1,2,0:T(8,128)S(1)} custom-call(f32[2,128,128]{2,1,0:T(8,128)S(1)} %get-tuple-element.24), custom_call_target="InvertDiagBlocksLowerTriangular" | custom-call | tf_op jit(solution)/shard_map/jit(_solve_triangular)/triangular_solve | solution.py:32
  230.4 2.5 fusion.3
  233.0 60.7 %all-reduce.16.cloned.1.call-done = f32[2,256,256]{1,2,0:T(8,128)} async-done(((f32[2,256,256]{1,2,0:T(8,128)}), f32[2,256,256]{1,2,0:T(8,128)}) %all-reduce.16.cloned.1.call-update) | async-done | bytes 524304 | tf_op jit(solution)/shard_map/psum | solution.py:11
  296.2 158.9 %all-reduce.30.cloned.1.call-done = (f32[2,1,256,256]{2,3,0,1:T(8,128)}, f32[2,1,256,256]{2,3,0,1:T(8,128)}, f32[2,1,256,256]{2,3,0,1:T(8,128)}, f32[2,1,256,256]{2,3,0,1:T(8,128)}) async-done(((f32[2,1,256,256]{2,3,0,1:T(8,128)}, f32[2,1,256,256]{2,3,0,1:T(8,128)}, f32[2,1,256,256]{2,3,0,1:T(8,128)}, f32[2,1,256,256]{2,3,0,1:T(8,128)}), (f32[2,1,256,256]{2,3,0,1:T(8,128)}, f32[2,1,256,256]{2,3,0,1:T(8,128)}, ...) | async-done | bytes 2097168 | tf_op jit(solution)/shard_map/psum | solution.py:11
  458.7 6.2 convolution_subtract_fusion.1
  467.9 142.9 %all-reduce.18.cloned.1.call-done = f32[256,256]{0,1:T(8,128)} async-done(((f32[256,256]{0,1:T(8,128)}), f32[256,256]{0,1:T(8,128)}) %all-reduce.18.cloned.1.call-update) | async-done | bytes 262160 | tf_op jit(solution)/shard_map/psum | solution.py:11
  612.8 11.7 cholesky.206
  624.6 9.8 custom-call.17
  634.9 11.7 cholesky.223
  649.4 4.3 while.7
  653.7 19.7 %custom-call.18 = f32[2,128,128]{1,2,0:T(8,128)S(1)} custom-call(f32[2,128,128]{2,1,0:T(8,128)S(1)} %get-tuple-element.25), custom_call_target="InvertDiagBlocksLowerTriangular" | custom-call | tf_op jit(solution)/shard_map/jit(_solve_triangular)/triangular_solve | solution.py:32
  674.3 2.5 fusion.1
  676.9 60.7 %all-reduce.20.cloned.1.call-done = f32[2,256,256]{1,2,0:T(8,128)} async-done(((f32[2,256,256]{1,2,0:T(8,128)}), f32[2,256,256]{1,2,0:T(8,128)}) %all-reduce.20.cloned.1.call-update) | async-done | bytes 524304 | tf_op jit(solution)/shard_map/psum | solution.py:11
  740.1 158.7 %all-reduce.28.cloned.1.call-done = (f32[2,1,256,256]{2,3,0,1:T(8,128)}, f32[2,1,256,256]{2,3,0,1:T(8,128)}, f32[2,1,256,256]{2,3,0,1:T(8,128)}, f32[2,1,256,256]{2,3,0,1:T(8,128)}) async-done(((f32[2,1,256,256]{2,3,0,1:T(8,128)}, f32[2,1,256,256]{2,3,0,1:T(8,128)}, f32[2,1,256,256]{2,3,0,1:T(8,128)}, f32[2,1,256,256]{2,3,0,1:T(8,128)}), (f32[2,1,256,256]{2,3,0,1:T(8,128)}, f32[2,1,256,256]{2,3,0,1:T(8,128)}, ...) | async-done | bytes 2097168 | tf_op jit(solution)/shard_map/psum | solution.py:11
  902.4 6.2 convolution_subtract_fusion
  911.7 142.8 %all-reduce.22.cloned.1.call-done = f32[256,256]{0,1:T(8,128)} async-done(((f32[256,256]{0,1:T(8,128)}), f32[256,256]{0,1:T(8,128)}) %all-reduce.22.cloned.1.call-update) | async-done | bytes 262160 | tf_op jit(solution)/shard_map/psum | solution.py:11
  1056.6 11.7 cholesky.240
  1068.4 9.8 custom-call.19
  1078.7 11.7 cholesky.257
  1093.2 4.4 while.8
  1097.6 19.7 %custom-call.20 = f32[2,128,128]{1,2,0:T(8,128)S(1)} custom-call(f32[2,128,128]{2,1,0:T(8,128)S(1)} %get-tuple-element.26), custom_call_target="InvertDiagBlocksLowerTriangular" | custom-call | tf_op jit(solution)/shard_map/jit(_solve_triangular)/triangular_solve | solution.py:32
  1118.1 2.5 fusion
  1120.7 60.7 %all-reduce.24.cloned.1.call-done = f32[2,256,256]{1,2,0:T(8,128)} async-done(((f32[2,256,256]{1,2,0:T(8,128)}), f32[2,256,256]{1,2,0:T(8,128)}) %all-reduce.24.cloned.1.call-update) | async-done | bytes 524304 | tf_op jit(solution)/shard_map/psum | solution.py:11
  1185.6 156.5 %all-reduce.26.cloned.1.call-done = (f32[2,1,256,256]{2,3,0,1:T(8,128)}, f32[2,1,256,256]{2,3,0,1:T(8,128)}, f32[2,1,256,256]{2,3,0,1:T(8,128)}, f32[2,1,256,256]{2,3,0,1:T(8,128)}) async-done(((f32[2,1,256,256]{2,3,0,1:T(8,128)}, f32[2,1,256,256]{2,3,0,1:T(8,128)}, f32[2,1,256,256]{2,3,0,1:T(8,128)}, f32[2,1,256,256]{2,3,0,1:T(8,128)}), (f32[2,1,256,256]{2,3,0,1:T(8,128)}, f32[2,1,256,256]{2,3,0,1:T(8,128)}, ...) | async-done | bytes 2097168 | tf_op jit(solution)/shard_map/psum | solution.py:11
  1345.7 7.3 subtract_bitcast_fusion
  1353.0 10.9 copy.38
  (112 shorter events, 54.2 us)
Async XLA Ops:
  7.2 160.0 %all-reduce.14.cloned.1.call-start = ((), (), s32[]{:S(2)}) async-start(), calls=%async_computation | async-start | bytes 524288 | tf_op jit(solution)/shard_map/psum | solution.py:11
  19.8 273.9 %all-reduce.16.cloned.1.call-start = ((), (), s32[]{:S(2)}) async-start(), calls=%async_computation.1 | async-start | bytes 1048576 | tf_op jit(solution)/shard_map/psum | solution.py:11
  232.9 222.1 %all-reduce.30.cloned.1.call-start = ((), (), s32[]{:S(2)}) async-start(), calls=%async_computation.8 | async-start | bytes 4194304 | tf_op jit(solution)/shard_map/psum | solution.py:11
  296.1 314.6 %all-reduce.18.cloned.1.call-start = ((), (), s32[]{:S(2)}) async-start(), calls=%async_computation.2 | async-start | bytes 524288 | tf_op jit(solution)/shard_map/psum | solution.py:11
  456.8 1.9 copy-start.2
  464.9 2.0 copy-start.1
  467.7 269.9 %all-reduce.20.cloned.1.call-start = ((), (), s32[]{:S(2)}) async-start(), calls=%async_computation.3 | async-start | bytes 1048576 | tf_op jit(solution)/shard_map/psum | solution.py:11
  676.8 222.0 %all-reduce.28.cloned.1.call-start = ((), (), s32[]{:S(2)}) async-start(), calls=%async_computation.7 | async-start | bytes 4194304 | tf_op jit(solution)/shard_map/psum | solution.py:11
  740.0 314.5 %all-reduce.22.cloned.1.call-start = ((), (), s32[]{:S(2)}) async-start(), calls=%async_computation.4 | async-start | bytes 524288 | tf_op jit(solution)/shard_map/psum | solution.py:11
  900.6 1.9 copy-start.3
  908.6 2.0 copy-start
  911.4 270.0 %all-reduce.24.cloned.1.call-start = ((), (), s32[]{:S(2)}) async-start(), calls=%async_computation.5 | async-start | bytes 1048576 | tf_op jit(solution)/shard_map/psum | solution.py:11
  1120.7 221.4 %all-reduce.26.cloned.1.call-start = ((), (), s32[]{:S(2)}) async-start(), calls=%async_computation.6 | async-start | bytes 4194304 | tf_op jit(solution)/shard_map/psum | solution.py:11
  1181.4 2.5 copy-start.4
  1343.8 1.9 copy-start.5
Sparse Core Ops, SparseCore 0:
  19.9 147.1 all-reduce.13
  233.1 60.5 all-reduce.15
  298.2 156.8 all-reduce.29
  467.8 142.9 all-reduce.17
  676.9 60.6 all-reduce.19
  741.9 156.8 all-reduce.27
  911.5 142.9 all-reduce.21
  1120.8 60.5 all-reduce.23
  1185.4 156.6 all-reduce.25
where the time goes:
time: 1380 us; the launch traced here: 1370 us
  waiting for transfers between devices  1090 us (79%)
  other arithmetic  181 us (13%)
  local copies, waits for them, and re-layouts  48.6 us (4%)
  matrix products  31.1 us (2%)
  between operations  18.8 us (1%)
    psum x9, waiting for transfers between devices, from_root(): return lax.psum(jnp.where(mine, shard, jnp.zeros_like(shard)), axis)  1090 us
    another operation x20, other arithmetic, body(): lower = jnp.linalg.cholesky(corner)  103 us
    another operation x7, other arithmetic, body(): jax.scipy.linalg.solve_triangular(lower, jnp.eye(tile, dtype=jnp.float32)...  59.1 us
  transfers between devices with their start and end apart: 9, of which 9 were waited for; matrix products, arithmetic and copies ran while one was open for 0% of the time, Pallas kernels for 0%

commit v1 on v0

v1 whole, which is shorter than its diff:
```python
import jax
import jax.numpy as jnp
from jax import lax
from jax.experimental import pallas as pl
from jax.experimental.pallas import tpu as pltpu
from jax.sharding import PartitionSpec as P

PANELS = 3
HI = lax.Precision.HIGHEST
N=768; NB=128

def dotg(a,b,ca,cb,prec=HI):
    return lax.dot_general(a,b,(((ca,),(cb,)),((),())),precision=prec,preferred_element_type=jnp.float32)


def factor128(load, store_l):
    sub = lax.broadcasted_iota(jnp.int32,(8,128),0)
    lane = lax.broadcasted_iota(jnp.int32,(8,128),1)
    full=(8,128)
    bc=lambda v: jnp.broadcast_to(v,full)
    S=[load(g) for g in range(16)]
    X=[jnp.where(lane==sub+8*g,1.0,0.0).astype(jnp.float32) for g in range(16)]
    for g in range(16):
        V=S[g]; XV=X[g]
        col=[bc(V[:,8*g+j:8*g+j+1]) for j in range(8)]
        a={(i,j):bc(col[j][i:i+1,:]) for j in range(8) for i in range(j,8)}
        y=[bc(V[i:i+1,:]) for i in range(8)]
        w=[bc(XV[i:i+1,:]) for i in range(8)]
        r=[None]*8; m={}
        XI=jnp.zeros(full,jnp.float32)
        for j in range(8):
            rs=lax.rsqrt(a[j,j]); r[j]=rs*rs
            XI=jnp.where(sub==j,w[j]*rs,XI)
            for i in range(j+1,8):
                m[i,j]=a[i,j]*r[j]
            for k in range(j+1,8):
                for i in range(k,8):
                    a[i,k]=a[i,k]-m[i,j]*a[k,j]
            for i in range(j+1,8):
                y[i]=y[i]-m[i,j]*y[j]
                w[i]=w[i]-m[i,j]*w[j]
        store_l(g,XI)
        if g<15:
            z=[None]*8; zx=[None]*8
            for j in range(7,-1,-1):
                z[j]=y[j]*r[j]; zx[j]=w[j]*r[j]
                for k in range(7,j,-1):
                    z[j]=z[j]-m[k,j]*z[k]; zx[j]=zx[j]-m[k,j]*zx[k]
            for h in range(g+1,16):
                s=S[h]; x=X[h]
                cb=[bc(s[:,8*g+j:8*g+j+1]) for j in range(8)]
                t=[cb[j]*z[j] for j in range(8)]
                tx=[cb[j]*zx[j] for j in range(8)]
                tree=lambda t:((t[0]+t[1])+(t[2]+t[3]))+((t[4]+t[5])+(t[6]+t[7]))
                S[h]=s-tree(t); X[h]=x-tree(tx)

def kern(c_ref, u_ref, x_ref, linv):
    r0=lax.broadcasted_iota(jnp.int32,(N,N),0); c0=lax.broadcasted_iota(jnp.int32,(N,N),1)
    u_ref[...]=c_ref[...]
    x_ref[...]=jnp.where(r0==c0,1.0,0.0).astype(jnp.float32)
    def step(t,_):
        o=pl.multiple_of(t*NB,NB)
        def load(g): return u_ref[pl.ds(pl.multiple_of(o+8*g,8),8), pl.ds(o,NB)]
        def store(g,v): linv[8*g:8*g+8,:]=v
        factor128(load,store)
        li=linv[...]
        ur=dotg(li,u_ref[pl.ds(o,NB),:],1,0)
        xr=dotg(li,x_ref[pl.ds(o,NB),:],1,0)
        u_ref[pl.ds(o,NB),:]=ur
        x_ref[pl.ds(o,NB),:]=xr
        for b in range(1,6):
            @pl.when(b>t)
            def _():
                ub=u_ref[pl.ds(o,NB), b*NB:(b+1)*NB]
                u_ref[b*NB:(b+1)*NB,:]-=dotg(ub,ur,0,0)
                x_ref[b*NB:(b+1)*NB,:]-=dotg(ub,xr,0,0)
        return 0
    lax.fori_loop(0,6,step,0)

def chol(c):
    return pl.pallas_call(kern,out_shape=(jax.ShapeDtypeStruct((N,N),jnp.float32),)*2,
      in_specs=[pl.BlockSpec(memory_space=pltpu.VMEM)],
      out_specs=(pl.BlockSpec(memory_space=pltpu.VMEM),)*2,
      scratch_shapes=[pltpu.VMEM((NB,NB),jnp.float32)],
      compiler_params=pltpu.CompilerParams(vmem_limit_bytes=48<<20))(c)
MESH = pl.DeviceIdType.MESH
CORNER = ((0, 0), (1, 0), (1, 1), (2, 0), (2, 1), (2, 2))
PIECES = 48


def comm_kernel(a0, A, B, C, asend, arecv, ysend, crecv, csend, psend, precv, brecv, bsend, loc):
    p = lax.axis_index("row")
    q = lax.axis_index("col")
    x = p // 8
    z = p % 8
    core = q % 2
    partner = q + 1 - 2 * core

    def at(px, pz):
        return (lax.rem(px + 4, 4) * 8 + lax.rem(pz + 8, 8), q)

    def along(d):
        return (p, lax.rem(q + d, 8))

    def rcopy(src, dst, ss, rs, dev):
        return pltpu.make_async_remote_copy(
            src_ref=src, dst_ref=dst, send_sem=ss, recv_sem=rs, device_id=dev, device_id_type=MESH
        )

    def arrived(ref, sem):
        pltpu.make_async_copy(ref, ref, sem).wait()

    barrier = pltpu.get_barrier_semaphore()
    for d in range(1, 8):
        pl.semaphore_signal(barrier, inc=1, device_id=along(d), device_id_type=MESH)
    for dx, dz in ((1, 0), (-1, 0), (0, 1), (0, -1)):
        pl.semaphore_signal(barrier, inc=1, device_id=at(x + dx, z + dz), device_id_type=MESH)
    pl.semaphore_wait(barrier, 11)

    def quarter(c, u):
        return pl.ds(pl.multiple_of((c + 2 * u) * 64, 64), 64)

    def ycopy(idx, d, u):
        rows = quarter(lax.rem(q + d, 2), u)
        return rcopy(a0.at[0, rows, :], C.at[idx, rows, :], ysend.at[(d - 1) * 2 + u], crecv.at[idx, u], along(d))

    for idx, (i, j) in enumerate(CORNER):

        @pl.when((p == i) & (q == j))
        def _(idx=idx):
            pltpu.make_async_copy(a0.at[0], C.at[idx], loc.at[2]).start()
            for u in range(2):
                for d in range(1, 8):
                    ycopy(idx, d, u).start()
            pltpu.make_async_copy(a0.at[0], C.at[idx], loc.at[2]).wait()

    first = lax.rem(z - q + 8, 8)

    def acopy(k, a, d):
        return rcopy(a0.at[a], A.at[k, a], asend.at[a, d - 1], arecv.at[k, a], along(d))

    for k in range(3):

        @pl.when(q == k)
        def _(k=k):
            for a in range(2):
                pltpu.make_async_copy(a0.at[a], A.at[k, a], loc.at[a]).start()
            for now in (True, False):
                for a in range(2):
                    for d in range(1, 8):

                        @pl.when((d == first) if now else (d != first))
                        def _(a=a, d=d):
                            acopy(k, a, d).start()

    def hops(x0, z0, typ, sx, sz):
        dx = lax.rem(x - x0 + 4, 4)
        dz = lax.rem(sz * (z - z0) + 16, 8)
        cz = (typ == 1) | (dx == 0)
        cx = (typ == 0) | (dz == 0)
        return (
            ((x, z + sz), cz & (dz <= 3)),
            ((x, z - sz), cz & ((dz == 0) | (dz >= 6))),
            ((x + 1, z), cx & ((dx == 0) | ((dx == 1) & (sx == 1)))),
            ((x - 1, z), cx & ((dx == 0) | ((dx == 3) & (sx == 0)))),
        )

    def corner(e, end):
        idx, u = e // 2, e % 2
        i, j = CORNER[idx]
        ref = C.at[idx, quarter(core, u), :]
        other = C.at[idx, quarter(1 - core, u), :]
        mine = (p == i) & (q == j)
        its = (p == i) & (partner == j)
        if not end:

            @pl.when(jnp.logical_not(mine))
            def _():
                arrived(ref, crecv.at[idx, u])

        for n, (dev, cond) in enumerate(hops(0, i, u, idx % 2, 1)):

            @pl.when(cond)
            def _(n=n, dev=dev):
                c = rcopy(ref, ref, csend.at[e, n], crecv.at[idx, u], at(*dev))
                c.wait_send() if end else c.start()

        @pl.when(jnp.logical_not(its))
        def _():
            c = rcopy(ref, ref, psend.at[e], precv.at[e], (p, partner))
            c.wait_send() if end else c.start()

        if end:

            @pl.when(jnp.logical_not(mine))
            def _():
                arrived(other, precv.at[e])

    def piece(e, end):
        x0 = e % 4
        r = e // 4
        h = r % 2
        a = (r // 2) % 2
        k = r // 4
        typ = jnp.where((r * 2) % 5 < 2, 1, 0)
        root = (x0 == x) & (z == q)
        ref = B.at[x0, a, k, pl.ds(pl.multiple_of(h * 128, 128), 128), :]
        if not end:

            @pl.when(root & (h == 0))
            def _():
                @pl.when(q == k)
                def _():
                    arrived(A.at[k, a], loc.at[a])

                @pl.when(q != k)
                def _():
                    arrived(A.at[k, a], arecv.at[k, a])

                c = pltpu.make_async_copy(A.at[k, a], B.at[x0, a, k], loc.at[3])
                c.start()
                c.wait()

            @pl.when(jnp.logical_not(root))
            def _():
                arrived(ref, brecv.at[e])

        for n, (dev, cond) in enumerate(hops(x0, q, typ, r % 2, 1 - 2 * ((r // 2) % 2))):

            @pl.when(cond)
            def _(n=n, dev=dev):
                c = rcopy(ref, ref, bsend.at[e, n], brecv.at[e], at(*dev))
                c.wait_send() if end else c.start()

    for e in range(12):
        corner(e, False)

    def go(e, _):
        piece(e, False)
        return 0

    lax.fori_loop(0, PIECES, go, 0)

    for k in range(3):
        for a in range(2):

            @pl.when((z != q) & (q == k))
            def _(k=k, a=a):
                arrived(A.at[k, a], loc.at[a])

            @pl.when((z != q) & (q != k))
            def _(k=k, a=a):
                arrived(A.at[k, a], arecv.at[k, a])

    for e in range(12):
        corner(e, True)

    def done(e, _):
        piece(e, True)
        return 0

    lax.fori_loop(0, PIECES, done, 0)

    for idx, (i, j) in enumerate(CORNER):

        @pl.when((p == i) & (q == j))
        def _(idx=idx):
            for d in range(1, 8):
                for u in range(2):
                    ycopy(idx, d, u).wait_send()

    for k in range(3):

        @pl.when(q == k)
        def _(k=k):
            for a in range(2):
                for d in range(1, 8):
                    acopy(k, a, d).wait_send()


def gather(a0):
    f32 = jnp.float32
    dma = pltpu.SemaphoreType.DMA
    return pl.pallas_call(
        comm_kernel,
        out_shape=(
            jax.ShapeDtypeStruct((3, 2, 256, 256), f32),
            jax.ShapeDtypeStruct((4, 2, 3, 256, 256), f32),
            jax.ShapeDtypeStruct((6, 256, 256), f32),
        ),
        in_specs=[pl.BlockSpec(memory_space=pltpu.VMEM)],
        out_specs=(pl.BlockSpec(memory_space=pltpu.VMEM),) * 3,
        scratch_shapes=[
            dma((2, 7)), dma((3, 2)), dma((14,)), dma((6, 2)), dma((12, 4)), dma((12,)), dma((12,)),
            dma((PIECES,)), dma((PIECES, 4)), dma((4,)),
        ],
        compiler_params=pltpu.CompilerParams(collective_id=0, has_side_effects=True, vmem_limit_bytes=40 << 20),
    )(a0)


def body(matrix):
    my_row = lax.axis_index("row")
    tile = matrix.shape[2]
    work = matrix.reshape(2, tile, 8, tile)
    A, B, C = gather(work[:, :, 0, :])
    t = lambda v: v.T
    corner = jnp.block([[C[0], t(C[1]), t(C[3])], [C[1], C[2], t(C[4])], [C[3], C[4], C[5]]])
    _, inv = chol(corner)
    inv = inv.reshape(3, 256, 3, 256)
    row_tiles = jnp.arange(2) * 32 + my_row
    panel = jnp.einsum("maik,njmk->ainj", A, inv, precision=HI)
    panel = jnp.where((row_tiles[:, None] >= jnp.arange(3))[:, None, :, None], panel, 0.0)
    turns = jnp.arange(4) * 8 + lax.axis_index("col")
    tiles = jnp.arange(2)[:, None] * 32 + turns
    mirrored = jnp.einsum("tamik,njmk->atinj", B, inv, precision=HI)
    mirrored = jnp.where((tiles[:, :, None] >= jnp.arange(3))[:, :, None, :, None], mirrored, 0.0)
    mirrored = mirrored.reshape(8, 256, 3, 256)
    work = work - jnp.einsum("ainj,clnj->aicl", panel, mirrored, precision=HI)
    return (work.reshape(matrix.shape), panel.reshape(2, 1, tile, PANELS * tile))


def solution(mesh):
    in_specs = (P(None, "row", None, None, "col", None),)
    out_specs = (P(None, "row", None, None, "col", None), P(None, "row", None, None))
    return jax.shard_map(body, mesh=mesh, in_specs=in_specs, out_specs=out_specs, check_vma=False)
```

time: 1380 us -> 457 us (0.33)
  waiting for transfers between devices: 1090 us -> 0 us
  Pallas kernels: 0 us -> 371 us
  other arithmetic: 181 us -> 1.71 us
  matrix products: 31.1 us -> 50.4 us
  local copies, waits for them, and re-layouts: 48.6 us -> 30 us
  between operations: 18.8 us -> 1.02 us
    psum x9 -> x0, waiting for transfers between devices: 1090 us -> none  [from_root(): return lax.psum(jnp.where(mine, shard, jnp.zeros_like(shard)), axis)]
    pallas_call x0 -> x2, Pallas kernels: none -> 371 us  [the longest x1 315 us: gather(): pl.pallas_call(comm_kernel, out_shape=(jax.ShapeDtypeStruct((3, 2, 256, 2...]
    another operation x33 -> x0, other arithmetic: 175 us -> none  [the longest x20 103 us: body(): lower = jnp.linalg.cholesky(corner)]
    dot_general x6 -> x3, matrix products: 27.1 us -> 50.4 us  [the longest x1 23.7 us: body(): work = work - jnp.einsum('ainj,clnj->aicl', panel, mirrored, precision=HI)]
    another operation x31 -> x0, local copies, waits for them, and re-layouts: 18 us -> none  [the longest x22 12.3 us: body(): jax.scipy.linalg.solve_triangular(lower, jnp.eye(tile, dtype=jnp.float32)...]
  transfers between devices with their start and end apart: 9 -> 0, of which waited for: 9 -> 0; matrix products, arithmetic and copies ran while one was open for 0% -> 0% of each run, Pallas kernels for 0% -> 0%
where the time goes in v1:
time: 457 us; the launch traced here: 454 us
  Pallas kernels  371 us (81%)
  matrix products  50.4 us (11%)
  local copies, waits for them, and re-layouts  30 us (7%)
    pallas_call x1, Pallas kernels, gather(): pl.pallas_call(comm_kernel, out_shape=(jax.ShapeDtypeStruct((3, 2, 256, 2...  315 us
    pallas_call x1, Pallas kernels, chol(): pl.pallas_call(kern, out_shape=(jax.ShapeDtypeStruct((N, N), jnp.float32)...  55.5 us
    dot_general x1, matrix products, body(): work = work - jnp.einsum('ainj,clnj->aicl', panel, mirrored, precision=HI)  23.7 us
    dot_general x1, matrix products, body(): mirrored = jnp.einsum('tamik,njmk->atinj', B, inv, precision=HI)  19 us
    unnamed x15, local copies, waits for them, and re-layouts  17.2 us

profile of v1, /device:TPU:18, one launch (start us, length us, event | category | flops | bytes accessed | tf_op | source)
XLA Modules:
  0.0 453.6 jit_solution(7470572158444947128)
XLA Ops:
  0.6 3.5 copy.61
  4.2 315.0 %shard_map.30 = (f32[3,2,256,256]{3,2,1,0:T(8,128)S(1)}, f32[4,2,3,256,256]{4,3,2,1,0:T(8,128)S(1)}, f32[6,256,256]{2,1,0:T(8,128)S(1)}) custom-call(f32[2,256,256]{2,1,0:T(8,128)S(1)} %slice_bitcast_fusion.a0), custom_call_target="tpu_custom_call" | custom-call | tf_op jit(solution)/shard_map/pallas_call | solution.py:284
  319.2 0.0 copy-start
  319.2 2.7 copy-done
  321.9 0.0 copy-start.1
  321.9 1.1 copy-done.1
  323.0 0.5 copy.16
  323.5 0.9 slice_bitcast_fusion.6
  324.4 0.0 copy-start.5
  324.4 0.0 copy-start.4
  324.4 0.1 slice_bitcast_fusion.3
  324.5 0.1 pad_maximum_fusion
  324.6 0.3 copy.20
  324.8 0.5 copy-done.5
  325.3 0.1 copy.19
  325.5 0.0 copy-done.4
  325.5 1.6 maximum_maximum_fusion.c_ref
  327.1 55.5 %shard_map.31 = (f32[768,768]{1,0:T(8,128)}, f32[768,768]{1,0:T(8,128)S(1)}) custom-call(f32[768,768]{1,0:T(8,128)} %maximum_maximum_fusion.c_ref), custom_call_target="tpu_custom_call" | custom-call | tf_op jit(solution)/shard_map/pallas_call | solution.py:81
  382.6 2.9 reshape.83
  385.5 0.0 copy-start.2
  385.5 7.7 %bitcast_select_fusion.1 = f32[2,256,3,256]{1,3,0,2:T(8,128)} fusion(f32[3,2,256,256]{3,2,1,0:T(8,128)} %copy-done.1, f32[3,256,3,256,1]{3,2,1,0,4:T(4,128)} %bitcast.71, pred[2,3]{0,1:T(4,128)(4,1)S(1)} %iota_compare_fusion.1), kind=kOutput, calls=%fused_computation.10 | convolution fusion | flops 3624271872 | bytes 5505030 | tf_op jit(solution)/shard_map/maik,njmk->ainj/dot_general | solution.py:311
  393.2 0.1 broadcast_add_fusion
  393.3 0.0 copy-done.2
  393.3 19.0 %bitcast_select_fusion = f32[2,4,256,3,256]{2,4,0,1,3:T(8,128)} fusion(pred[2,4,3]{0,1,2:T(4,128)(4,1)S(1)} %iota_compare_fusion, f32[4,2,3,256,256]{4,3,2,1,0:T(8,128)} %copy-done, f32[3,256,3,256,1,1]{3,2,1,0,5,4:T(4,128)S(1)} %bitcast.72), kind=kOutput, calls=%fused_computation | convolution fusion | flops 14497087488 | bytes 14942232 | tf_op jit(solution)/shard_map/tamik,njmk->atinj/dot_general | solution.py:315
  412.3 0.0 copy-start.3
  412.3 6.7 %copy.24 = f32[2,4,256,3,256]{4,2,3,1,0:T(8,128)} copy(f32[2,4,256,3,256]{2,4,0,1,3:T(8,128)} %bitcast_select_fusion) | data formatting | bytes 12582912 | tf_op jit(solution)/shard_map/jit(_where)/select_n | solution.py:316
  419.0 0.0 copy-done.3
  419.0 23.7 %fusion.2 = f32[2,1,256,8,1,256]{5,2,0,3,4,1:T(8,128)S(1)} fusion(f32[8,256,3,256,1]{3,1,4,2,0:T(8,128)} %bitcast.70, f32[2,256,3,256]{1,3,0,2:T(8,128)S(1)} %copy-done.3, f32[2,1,256,8,1,256]{5,4,3,2,1,0:T(1,128)} %param.1), kind=kOutput, calls=%fused_computation.4 | convolution fusion | flops 9664724992 | bytes 16252928 | tf_op jit(solution)/shard_map/ainj,clnj->aicl/dot_general | solution.py:318
  442.7 6.3 %copy.28 = f32[2,1,256,8,1,256]{5,4,3,2,1,0:T(1,128)} copy(f32[2,1,256,8,1,256]{5,2,0,3,4,1:T(8,128)S(1)} %fusion.2) | data formatting | bytes 8388608
  449.0 1.3 copy.27
  450.3 3.0 copy.29
  (6 shorter events, 0.1 us)
Async XLA Ops:
  319.2 2.7 copy-start
  321.9 1.1 copy-start.1
  324.4 0.9 copy-start.5
  324.4 1.1 copy-start.4
  385.5 7.8 %copy-start.2 = (f32[3,256,3,256]{3,2,1,0:T(4,128)S(1)}, f32[3,256,3,256]{3,2,1,0:T(4,128)}, u32[]{:S(2)}) copy-start(f32[3,256,3,256]{3,2,1,0:T(4,128)} %reshape.83) | copy-start | bytes 7077892
  412.3 6.7 %copy-start.3 = (f32[2,256,3,256]{1,3,0,2:T(8,128)S(1)}, f32[2,256,3,256]{1,3,0,2:T(8,128)}, u32[]{:S(2)}) copy-start(f32[2,256,3,256]{1,3,0,2:T(8,128)} %bitcast_select_fusion.1) | copy-start | bytes 4718596

commit v2 on v1

v2 whole, which is shorter than its diff:
```python
import jax
import jax.numpy as jnp
from jax import lax
from jax.experimental import pallas as pl
from jax.experimental.pallas import tpu as pltpu
from jax.sharding import PartitionSpec as P

HI = lax.Precision.HIGHEST


def dots(a, b, dim, precision=HI):
    return lax.dot_general(a, b, (((1,), (dim,)), ((), ())), precision=precision, preferred_element_type=jnp.float32)


def tdot(a, b):
    return dots(a, b, 1)


def ndot(a, b):
    return dots(a, b, 0)


def factor128(load, store_l, poll):
    sub = lax.broadcasted_iota(jnp.int32,(8,128),0)
    lane = lax.broadcasted_iota(jnp.int32,(8,128),1)
    full=(8,128)
    bc=lambda v: jnp.broadcast_to(v,full)
    S=[load(g) for g in range(16)]
    X=[jnp.where(lane==sub+8*g,1.0,0.0).astype(jnp.float32) for g in range(16)]
    for g in range(16):
        V=S[g]; XV=X[g]
        col=[bc(V[:,8*g+j:8*g+j+1]) for j in range(8)]
        a={(i,j):bc(col[j][i:i+1,:]) for j in range(8) for i in range(j,8)}
        y=[bc(V[i:i+1,:]) for i in range(8)]
        w=[bc(XV[i:i+1,:]) for i in range(8)]
        r=[None]*8; m={}
        XI=jnp.zeros(full,jnp.float32)
        for j in range(8):
            rs=lax.rsqrt(a[j,j]); r[j]=rs*rs
            XI=jnp.where(sub==j,w[j]*rs,XI)
            for i in range(j+1,8):
                m[i,j]=a[i,j]*r[j]
            for k in range(j+1,8):
                for i in range(k,8):
                    a[i,k]=a[i,k]-m[i,j]*a[k,j]
            for i in range(j+1,8):
                y[i]=y[i]-m[i,j]*y[j]
                w[i]=w[i]-m[i,j]*w[j]
        store_l(g,XI)
        if g==7:
            poll()
        if g<15:
            z=[None]*8; zx=[None]*8
            for j in range(7,-1,-1):
                z[j]=y[j]*r[j]; zx[j]=w[j]*r[j]
                for k in range(7,j,-1):
                    z[j]=z[j]-m[k,j]*z[k]; zx[j]=zx[j]-m[k,j]*zx[k]
            for h in range(g+1,16):
                s=S[h]; x=X[h]
                cb=[bc(s[:,8*g+j:8*g+j+1]) for j in range(8)]
                t=[cb[j]*z[j] for j in range(8)]
                tx=[cb[j]*zx[j] for j in range(8)]
                tree=lambda t:((t[0]+t[1])+(t[2]+t[3]))+((t[4]+t[5])+(t[6]+t[7]))
                S[h]=s-tree(t); X[h]=x-tree(tx)

MESH = pl.DeviceIdType.MESH
CORNER = ((0, 0), (1, 0), (1, 1), (2, 0), (2, 1), (2, 2))
PIECES = 48


def comm_kernel(mat, A, B, V, a0, C, W, M, tile, dref, lref, l0, m0, asend, arecv, ysend, crecv, csend, psend, precv, brecv, bsend, loc):
    p = lax.axis_index("row")
    q = lax.axis_index("col")
    x = p // 8
    z = p % 8
    core = q % 2
    partner = q + 1 - 2 * core

    def at(px, pz):
        return (lax.rem(px + 4, 4) * 8 + lax.rem(pz + 8, 8), q)

    def along(d):
        return (p, lax.rem(q + d, 8))

    def rcopy(src, dst, ss, rs, dev):
        return pltpu.make_async_remote_copy(
            src_ref=src, dst_ref=dst, send_sem=ss, recv_sem=rs, device_id=dev, device_id_type=MESH
        )

    def arrived(ref, sem):
        pltpu.make_async_copy(ref, ref, sem).wait()

    for a in range(2):
        pltpu.make_async_copy(mat.at[a, 0, :, 0, 0, :], a0.at[a], loc.at[4 + a]).start()

    barrier = pltpu.get_barrier_semaphore()
    for d in range(1, 8):
        pl.semaphore_signal(barrier, inc=1, device_id=along(d), device_id_type=MESH)
    for dx, dz in ((1, 0), (-1, 0), (0, 1), (0, -1)):
        pl.semaphore_signal(barrier, inc=1, device_id=at(x + dx, z + dz), device_id_type=MESH)
    pl.semaphore_wait(barrier, 11)
    for a in range(2):
        arrived(a0.at[a], loc.at[4 + a])

    def quarter(c, u):
        return pl.ds(pl.multiple_of((c + 2 * u) * 64, 64), 64)

    def ycopy(idx, d, u):
        rows = quarter(lax.rem(q + d, 2), u)
        return rcopy(a0.at[0, rows, :], C.at[idx, rows, :], ysend.at[(d - 1) * 2 + u], crecv.at[idx, u], along(d))

    for idx, (i, j) in enumerate(CORNER):

        @pl.when((p == i) & (q == j))
        def _(idx=idx):
            pltpu.make_async_copy(a0.at[0], C.at[idx], loc.at[2]).start()
            for u in range(2):
                for d in range(1, 8):
                    ycopy(idx, d, u).start()
            pltpu.make_async_copy(a0.at[0], C.at[idx], loc.at[2]).wait()

    first = lax.rem(z - q + 8, 8)

    def acopy(k, a, d):
        return rcopy(a0.at[a], A.at[k, a], asend.at[a, d - 1], arecv.at[k, a], along(d))

    for k in range(3):

        @pl.when(q == k)
        def _(k=k):
            for a in range(2):
                pltpu.make_async_copy(a0.at[a], A.at[k, a], loc.at[a]).start()
            for now in (True, False):
                for a in range(2):
                    for d in range(1, 8):

                        @pl.when((d == first) if now else (d != first))
                        def _(a=a, d=d):
                            acopy(k, a, d).start()

    def hops(x0, z0, typ, sx, sz):
        dx = lax.rem(x - x0 + 4, 4)
        dz = lax.rem(sz * (z - z0) + 16, 8)
        cz = (typ == 1) | (dx == 0)
        cx = (typ == 0) | (dz == 0)
        return (
            ((x, z + sz), cz & (dz <= 3)),
            ((x, z - sz), cz & ((dz == 0) | (dz >= 6))),
            ((x + 1, z), cx & ((dx == 0) | ((dx == 1) & (sx == 1)))),
            ((x - 1, z), cx & ((dx == 0) | ((dx == 3) & (sx == 0)))),
        )

    def corner(e, end):
        idx, u = e // 2, e % 2
        i, j = CORNER[idx]
        ref = C.at[idx, quarter(core, u), :]
        other = C.at[idx, quarter(1 - core, u), :]
        mine = (p == i) & (q == j)
        its = (p == i) & (partner == j)
        if end is False:

            @pl.when(jnp.logical_not(mine))
            def _():
                arrived(ref, crecv.at[idx, u])

        if end is not None:

            for n, (dev, cond) in enumerate(hops(0, i, u, idx % 2, 1)):

                @pl.when(cond)
                def _(n=n, dev=dev):
                    c = rcopy(ref, ref, csend.at[e, n], crecv.at[idx, u], at(*dev))
                    c.wait_send() if end else c.start()

            @pl.when(jnp.logical_not(its))
            def _():
                c = rcopy(ref, ref, psend.at[e], precv.at[e], (p, partner))
                c.wait_send() if end else c.start()

        if end is None:

            @pl.when(jnp.logical_not(mine))
            def _():
                arrived(other, precv.at[e])

    dz = lax.rem(z - q + 8, 8)
    root = dz == 0

    def half(x0, r):
        h = r % 2
        a = (r // 2) % 2
        k = r // 4
        return B.at[x0, a, k, pl.ds(pl.multiple_of(h * 128, 128), 128), :]

    def send(x0, r, n, dev, cond, end):
        e = x0 * 12 + r

        @pl.when(cond)
        def _():
            c = rcopy(half(x0, r), half(x0, r), bsend.at[e, n], brecv.at[e], at(*dev))
            c.wait_send() if end else c.start()

    def own(r, end):
        a = (r // 2) % 2
        k = r // 4
        if not end:

            @pl.when(root & (r % 2 == 0))
            def _():
                @pl.when(q == k)
                def _():
                    arrived(A.at[k, a], loc.at[a])

                @pl.when(q != k)
                def _():
                    arrived(A.at[k, a], arecv.at[k, a])

                c = pltpu.make_async_copy(A.at[k, a], B.at[x, a, k], loc.at[3])
                c.start()
                c.wait()

            @pl.when(jnp.logical_not(root))
            def _():
                arrived(half(x, r), brecv.at[x * 12 + r])

        send(x, r, 0, (x, z + 1), dz <= 3, end)
        send(x, r, 1, (x, z - 1), root | (dz >= 6), end)
        send(x, r, 2, (x + 1, z), p >= 0, end)
        send(x, r, 3, (x - 1, z), p >= 0, end)

    left = lax.rem(x + 3, 4)
    right = lax.rem(x + 1, 4)
    across = lax.rem(x + 2, 4)

    def passing(r, end):
        if not end:
            arrived(half(left, r), brecv.at[left * 12 + r])
        send(left, r, 0, (x + 1, z), r % 2 == 0, end)
        if not end:
            arrived(half(right, r), brecv.at[right * 12 + r])
        send(right, r, 1, (x - 1, z), r % 2 == 1, end)


    def go(r, _):
        @pl.when(r < 12)
        def _():
            own(r, False)

        @pl.when(r > 0)
        def _():
            passing(r - 1, False)

        return 0


    for e in range(12):
        corner(e, False)
        if e % 3 == 2:
            go(e // 3, 0)
    for e in range(12):
        corner(e, None)

    tile[...] = C[0]
    dref[...] = tile[:128, :128]

    def step(t, _):
        def poll(r):
            @pl.when(r < 13)
            def _():
                go(r, 0)

        def load(g):
            return dref[8 * g : 8 * g + 8, :]

        def store(g, v):
            lref[8 * g : 8 * g + 8, :] = v

        poll(4 + 2 * t)
        factor128(load, store, lambda: poll(5 + 2 * t))

        @pl.when(t % 2 == 0)
        def _():
            li = lref[...]
            m = tdot(tile[128:, :128], li)
            l0[...] = li
            m0[...] = m
            dref[...] = tile[128:, 128:] - tdot(m, m)

        for k in range(3):

            @pl.when(t == 2 * k + 1)
            def _(k=k):
                o = 256 * k
                li = lref[...]
                V[o : o + 128, o : o + 128] = l0[...]
                V[o : o + 128, o + 128 : o + 256] = jnp.zeros((128, 128), jnp.float32)
                V[o + 128 : o + 256, o + 128 : o + 256] = li
                V[o + 128 : o + 256, o : o + 128] = -ndot(li, ndot(m0[...], l0[...]))
                v = V[o : o + 256, o : o + 256]
                if k == 0:
                    m1 = tdot(C[1], v)
                    m2 = tdot(C[3], v)
                    tile[...] = C[2] - tdot(m1, m1)
                    dref[...] = tile[:128, :128]
                    W[0] = C[4] - tdot(m2, m1)
                    W[1] = C[5] - tdot(m2, m2)
                    M[0] = ndot(m1, v)
                    M[1] = ndot(m2, v)
                if k == 1:
                    m = tdot(W[0], v)
                    tile[...] = W[1] - tdot(m, m)
                    dref[...] = tile[:128, :128]
                    V[256:512, :256] = -ndot(v, M[0])
                    M[1] += ndot(m, V[256:512, :256])
                    M[0] = ndot(m, v)
                if k == 2:
                    V[512:, :256] = -ndot(v, M[1])
                    V[512:, 256:512] = -ndot(v, M[0])

        return 0

    lax.fori_loop(0, 6, step, 0)

    def last(r, _):
        arrived(half(across, r), brecv.at[across * 12 + r])
        return 0

    lax.fori_loop(0, 12, last, 0)

    for k in range(3):
        for a in range(2):

            @pl.when((z != q) & (q == k))
            def _(k=k, a=a):
                arrived(A.at[k, a], loc.at[a])

            @pl.when((z != q) & (q != k))
            def _(k=k, a=a):
                arrived(A.at[k, a], arecv.at[k, a])

    for e in range(12):
        corner(e, True)

    def done(r, _):
        own(r, True)
        passing(r, True)
        return 0

    lax.fori_loop(0, 12, done, 0)

    for idx, (i, j) in enumerate(CORNER):

        @pl.when((p == i) & (q == j))
        def _(idx=idx):
            for d in range(1, 8):
                for u in range(2):
                    ycopy(idx, d, u).wait_send()

    for k in range(3):

        @pl.when(q == k)
        def _(k=k):
            for a in range(2):
                for d in range(1, 8):
                    acopy(k, a, d).wait_send()


def gather(matrix):
    f32 = jnp.float32
    dma = pltpu.SemaphoreType.DMA
    vm = pltpu.VMEM
    return pl.pallas_call(
        comm_kernel,
        out_shape=(
            jax.ShapeDtypeStruct((3, 2, 256, 256), f32),
            jax.ShapeDtypeStruct((4, 2, 3, 256, 256), f32),
            jax.ShapeDtypeStruct((768, 768), f32),
        ),
        in_specs=[pl.BlockSpec(memory_space=pl.ANY)],
        out_specs=(pl.BlockSpec(memory_space=vm),) * 3,
        scratch_shapes=[
            vm((2, 256, 256), f32), vm((6, 256, 256), f32), vm((2, 256, 256), f32), vm((2, 256, 256), f32),
            vm((256, 256), f32), vm((128, 128), f32), vm((128, 128), f32), vm((128, 128), f32), vm((128, 128), f32),
            dma((2, 7)), dma((3, 2)), dma((14,)), dma((6, 2)), dma((12, 4)), dma((12,)), dma((12,)),
            dma((PIECES,)), dma((PIECES, 4)), dma((6,)),
        ],
        compiler_params=pltpu.CompilerParams(collective_id=0, has_side_effects=True, vmem_limit_bytes=44 << 20),
    )(matrix)


def split(v):
    hi = v.astype(jnp.bfloat16)
    return hi, (v - hi.astype(jnp.float32)).astype(jnp.bfloat16)


def update_kernel(mat, A, B, V, out, panel, vh, vl, ph, plo):
    c = pl.program_id(0)
    p = lax.axis_index("row")
    q = lax.axis_index("col")

    def bdot(a, b):
        return lax.dot_general(a, b, (((1,), (1,)), ((), ())), preferred_element_type=jnp.float32)

    def rows(load, number, put):
        parts = [split(load(m)) for m in range(3)]
        for n in range(3):
            total = None
            for m in range(n + 1):
                h, l = parts[m]
                at = (slice(256 * n, 256 * n + 256), slice(256 * m, 256 * m + 256))
                term = bdot(h, vh[at]) + (bdot(h, vl[at]) + bdot(l, vh[at]))
                total = term if total is None else total + term
            put(n, jnp.where(number >= n, total, 0.0))

    @pl.when(c == 0)
    def _():
        for n in range(3):
            at = (slice(256 * n, 256 * n + 256), slice(0, 256 * n + 256))
            vh[at], vl[at] = split(V[at])
        for a in range(2):

            def put(n, value):
                panel[a, 0, :, 256 * n : 256 * n + 256] = value
                ph[a, :, 256 * n : 256 * n + 256], plo[a, :, 256 * n : 256 * n + 256] = split(value)

            rows(lambda m: A[m, a], a * 32 + p, put)

    mirrored = [None] * 3

    def keep(n, value):
        mirrored[n] = split(value)

    rows(lambda m: B[0, 0, m], c * 8 + q, keep)
    mh = jnp.concatenate([m[0] for m in mirrored], axis=1)
    ml = jnp.concatenate([m[1] for m in mirrored], axis=1)
    for a in range(2):
        term = bdot(ph[a], mh) + (bdot(ph[a], ml) + bdot(plo[a], mh))
        out[a, 0, :, 0, 0, :] = mat[a, 0, :, 0, 0, :] - term


def update(matrix, A, B, V):
    f32 = jnp.float32
    bf16 = jnp.bfloat16
    vm = pltpu.VMEM
    block = pl.BlockSpec((2, 1, 256, 1, 1, 256), lambda c: (0, 0, 0, c, 0, 0))
    return pl.pallas_call(
        update_kernel,
        grid=(8,),
        out_shape=(jax.ShapeDtypeStruct(matrix.shape, f32), jax.ShapeDtypeStruct((2, 1, 256, 768), f32)),
        in_specs=[
            block,
            pl.BlockSpec((3, 2, 256, 256), lambda c: (0, 0, 0, 0)),
            pl.BlockSpec((1, 1, 3, 256, 256), lambda c: (c % 4, c // 4, 0, 0, 0)),
            pl.BlockSpec((768, 768), lambda c: (0, 0)),
        ],
        out_specs=(block, pl.BlockSpec((2, 1, 256, 768), lambda c: (0, 0, 0, 0))),
        scratch_shapes=[vm((768, 768), bf16), vm((768, 768), bf16), vm((2, 256, 768), bf16), vm((2, 256, 768), bf16)],
        compiler_params=pltpu.CompilerParams(vmem_limit_bytes=44 << 20),
    )(matrix, A, B, V)


def body(matrix):
    A, B, V = gather(matrix)
    return update(matrix, A, B, V)


def solution(mesh):
    in_specs = (P(None, "row", None, None, "col", None),)
    out_specs = (P(None, "row", None, None, "col", None), P(None, "row", None, None))
    return jax.shard_map(body, mesh=mesh, in_specs=in_specs, out_specs=out_specs, check_vma=False)
```

time: 457 us -> 228 us (0.50)
  the two profiles are of different devices: /device:TPU:18 before, /device:TPU:90 now
where the time goes in v2:
time: 228 us
  Pallas kernels  225 us (99%)
    pallas_call x1, Pallas kernels, gather(): pl.pallas_call(comm_kernel, out_shape=(jax.ShapeDtypeStruct((3, 2, 256, 2...  207 us
    pallas_call x1, Pallas kernels, update(): pl.pallas_call(update_kernel, grid=(8,), out_shape=(jax.ShapeDtypeStruct(...  18.6 us

profile of v2, /device:TPU:90, one launch (start us, length us, event | category | flops | bytes accessed | tf_op | source)
XLA Modules:
  0.0 227.9 jit_solution(13469203644432070692)
XLA Ops:
  0.6 0.0 copy-start
  0.6 2.2 copy-done
  2.8 206.5 %shard_map.30 = (f32[3,2,256,256]{3,2,1,0:T(8,128)S(1)}, f32[4,2,3,256,256]{4,3,2,1,0:T(8,128)}, f32[768,768]{1,0:T(8,128)S(1)}) custom-call(f32[2,1,256,8,1,256]{5,4,3,2,1,0:T(1,128)S(1)} %copy-done), custom_call_target="tpu_custom_call" | custom-call | tf_op jit(solution)/shard_map/pallas_call | solution.py:372
  209.3 18.6 %shard_map.31 = (f32[2,1,256,8,1,256]{5,4,3,2,1,0:T(1,128)}, f32[2,1,256,768]{3,2,1,0:T(8,128)}) custom-call(f32[2,1,256,8,1,256]{5,4,3,2,1,0:T(1,128)S(1)} %copy-done, f32[3,2,256,256]{3,2,1,0:T(8,128)S(1)} %get-tuple-element.5.A, f32[4,2,3,256,256]{4,3,2,1,0:T(8,128)} %get-tuple-element.6.B, f32[768,768]{1,0:T(8,128)S(1)} %get-tuple-element.7.V), custom_call_target="tpu_custom_call" | custom-call | tf_op jit(solution)/shard_map/pallas_call | solution.py:446
Async XLA Ops:
  0.6 2.2 copy-start

commit v3 on v2

--- a/solution.py
+++ b/solution.py
@@ -47,8 +47,8 @@
                 y[i]=y[i]-m[i,j]*y[j]
                 w[i]=w[i]-m[i,j]*w[j]
         store_l(g,XI)
-        if g==7:
-            poll()
+        if g in POLLS:
+            poll(POLLS.index(g))
         if g<15:
             z=[None]*8; zx=[None]*8
             for j in range(7,-1,-1):
@@ -65,10 +65,11 @@
 
 MESH = pl.DeviceIdType.MESH
 CORNER = ((0, 0), (1, 0), (1, 1), (2, 0), (2, 1), (2, 2))
+POLLS = (5, 10)
 PIECES = 48
 
 
-def comm_kernel(mat, A, B, V, a0, C, W, M, tile, dref, lref, l0, m0, asend, arecv, ysend, crecv, csend, psend, precv, brecv, bsend, loc):
+def comm_kernel(mat, A, B, V, a0, C, W, M, tile, dref, lref, l0, m0, asend, arecv, ysend, crecv, csend, psend, precv, brecv, bsend, fsend, loc):
     p = lax.axis_index("row")
     q = lax.axis_index("col")
     x = p // 8
@@ -124,19 +125,37 @@
     def acopy(k, a, d):
         return rcopy(a0.at[a], A.at[k, a], asend.at[a, d - 1], arecv.at[k, a], along(d))
 
+    def direct(a, d):
+        to = lax.rem(q + d, 8)
+        return (to // 2 == q // 2) | (to % 2 == a)
+
+    def forward(k, end):
+        ref = A.at[k, core]
+
+        @pl.when(q // 2 != k // 2)
+        def _():
+            if not end:
+
+                @pl.when(z != q)
+                def _():
+                    arrived(ref, arecv.at[k, core])
+
+            @pl.when(partner != z)
+            def _():
+                c = rcopy(ref, ref, fsend.at[k], arecv.at[k, core], (p, partner))
+                c.wait_send() if end else c.start()
+
     for k in range(3):
 
         @pl.when(q == k)
         def _(k=k):
             for a in range(2):
                 pltpu.make_async_copy(a0.at[a], A.at[k, a], loc.at[a]).start()
-            for now in (True, False):
-                for a in range(2):
-                    for d in range(1, 8):
-
-                        @pl.when((d == first) if now else (d != first))
-                        def _(a=a, d=d):
-                            acopy(k, a, d).start()
+                for d in range(1, 8):
+
+                    @pl.when(d == first)
+                    def _(a=a, d=d):
+                        acopy(k, a, d).start()
 
     def hops(x0, z0, typ, sx, sz):
         dx = lax.rem(x - x0 + 4, 4)
@@ -200,33 +219,38 @@
             c = rcopy(half(x0, r), half(x0, r), bsend.at[e, n], brecv.at[e], at(*dev))
             c.wait_send() if end else c.start()
 
-    def own(r, end):
+    def emit(r, who, end):
+        send(x, r, 0, (x, z + 1), who & (dz <= 3), end)
+        send(x, r, 1, (x, z - 1), who & (root | (dz >= 6)), end)
+        send(x, r, 2, (x + 1, z), who, end)
+        send(x, r, 3, (x - 1, z), who, end)
+
+    def lead(r):
         a = (r // 2) % 2
         k = r // 4
-        if not end:
-
-            @pl.when(root & (r % 2 == 0))
-            def _():
-                @pl.when(q == k)
-                def _():
-                    arrived(A.at[k, a], loc.at[a])
-
-                @pl.when(q != k)
-                def _():
-                    arrived(A.at[k, a], arecv.at[k, a])
-
-                c = pltpu.make_async_copy(A.at[k, a], B.at[x, a, k], loc.at[3])
-                c.start()
-                c.wait()
-
-            @pl.when(jnp.logical_not(root))
-            def _():
-                arrived(half(x, r), brecv.at[x * 12 + r])
-
-        send(x, r, 0, (x, z + 1), dz <= 3, end)
-        send(x, r, 1, (x, z - 1), root | (dz >= 6), end)
-        send(x, r, 2, (x + 1, z), p >= 0, end)
-        send(x, r, 3, (x - 1, z), p >= 0, end)
+
+        @pl.when(root & (r % 2 == 0))
+        def _():
+            @pl.when(q == k)
+            def _():
+                arrived(A.at[k, a], loc.at[a])
+
+            @pl.when(q != k)
+            def _():
+                arrived(A.at[k, a], arecv.at[k, a])
+
+            c = pltpu.make_async_copy(A.at[k, a], B.at[x, a, k], loc.at[3])
+            c.start()
+            c.wait()
+
+        emit(r, root, False)
+
+    def own(r):
+        @pl.when(jnp.logical_not(root))
+        def _():
+            arrived(half(x, r), brecv.at[x * 12 + r])
+
+        emit(r, jnp.logical_not(root), False)
 
     left = lax.rem(x + 3, 4)
     right = lax.rem(x + 1, 4)
@@ -242,9 +266,13 @@
 
 
     def go(r, _):
+        @pl.when(r + 3 < 12)
+        def _():
+            lead(r + 3)
+
         @pl.when(r < 12)
         def _():
-            own(r, False)
+            own(r)
 
         @pl.when(r > 0)
         def _():
@@ -255,19 +283,37 @@
 
     for e in range(12):
         corner(e, False)
-        if e % 3 == 2:
-            go(e // 3, 0)
+        for r, after in enumerate((3, 7, 11)):
+            if e == after:
+                lead(r)
     for e in range(12):
         corner(e, None)
 
+    late = jnp.minimum(dz, 8 - dz)
     tile[...] = C[0]
     dref[...] = tile[:128, :128]
 
     def step(t, _):
         def poll(r):
-            @pl.when(r < 13)
+            @pl.when((r >= 0) & (r < 13))
             def _():
                 go(r, 0)
+
+        for k in range(3):
+            for a in range(2):
+
+                @pl.when((q == k) & (t == 0))
+                def _(k=k, a=a):
+                    for d in range(1, 8):
+
+                        @pl.when((d != first) & direct(a, d))
+                        def _(d=d):
+                            acopy(k, a, d).start()
+
+        @pl.when(t == 4)
+        def _():
+            for k in range(3):
+                forward(k, False)
 
         def load(g):
             return dref[8 * g : 8 * g + 8, :]
@@ -275,8 +321,8 @@
         def store(g, v):
             lref[8 * g : 8 * g + 8, :] = v
 
-        poll(4 + 2 * t)
-        factor128(load, store, lambda: poll(5 + 2 * t))
+        poll(3 * t - late)
+        factor128(load, store, lambda i: poll(1 + 3 * t + i - late))
 
         @pl.when(t % 2 == 0)
         def _():
@@ -320,6 +366,7 @@
         return 0
 
     lax.fori_loop(0, 6, step, 0)
+    lax.fori_loop(jnp.minimum(18 - late, 13), 13, go, 0)
 
     def last(r, _):
         arrived(half(across, r), brecv.at[across * 12 + r])
@@ -334,7 +381,7 @@
             def _(k=k, a=a):
                 arrived(A.at[k, a], loc.at[a])
 
-            @pl.when((z != q) & (q != k))
+            @pl.when((z != q) & (q != k) & ((q // 2 == k // 2) | (core != a)))
             def _(k=k, a=a):
                 arrived(A.at[k, a], arecv.at[k, a])
 
@@ -342,7 +389,7 @@
         corner(e, True)
 
     def done(r, _):
-        own(r, True)
+        emit(r, p >= 0, True)
         passing(r, True)
         return 0
 
@@ -362,7 +409,13 @@
         def _(k=k):
             for a in range(2):
                 for d in range(1, 8):
-                    acopy(k, a, d).wait_send()
+
+                    @pl.when((d == first) | direct(a, d))
+                    def _(a=a, d=d):
+                        acopy(k, a, d).wait_send()
+
+    for k in range(3):
+        forward(k, True)
 
 
 def gather(matrix):
@@ -382,7 +435,7 @@
             vm((2, 256, 256), f32), vm((6, 256, 256), f32), vm((2, 256, 256), f32), vm((2, 256, 256), f32),
             vm((256, 256), f32), vm((128, 128), f32), vm((128, 128), f32), vm((128, 128), f32), vm((128, 128), f32),
             dma((2, 7)), dma((3, 2)), dma((14,)), dma((6, 2)), dma((12, 4)), dma((12,)), dma((12,)),
-            dma((PIECES,)), dma((PIECES, 4)), dma((6,)),
+            dma((PIECES,)), dma((PIECES, 4)), dma((3,)), dma((6,)),
         ],
         compiler_params=pltpu.CompilerParams(collective_id=0, has_side_effects=True, vmem_limit_bytes=44 << 20),
     )(matrix)

time: 228 us -> 155 us (0.68)
  the two profiles are of different devices: /device:TPU:90 before, /device:TPU:18 now
where the time goes in v3:
time: 155 us
  Pallas kernels  152 us (98%)
  local copies, waits for them, and re-layouts  2.18 us (1%)
    pallas_call x1, Pallas kernels, gather(): pl.pallas_call(comm_kernel, out_shape=(jax.ShapeDtypeStruct((3, 2, 256, 2...  133 us
    pallas_call x1, Pallas kernels, update(): pl.pallas_call(update_kernel, grid=(8,), out_shape=(jax.ShapeDtypeStruct(...  18.7 us

profile of v3, /device:TPU:18, one launch (start us, length us, event | category | flops | bytes accessed | tf_op | source)
XLA Modules:
  0.0 154.6 jit_solution(4732785374422715786)
XLA Ops:
  0.6 0.0 copy-start
  0.6 2.2 %copy-done = f32[2,1,256,8,1,256]{5,4,3,2,1,0:T(1,128)S(1)} copy-done((f32[2,1,256,8,1,256]{5,4,3,2,1,0:T(1,128)S(1)}, f32[2,1,256,8,1,256]{5,4,3,2,1,0:T(1,128)}, u32[]{:S(2)}) %copy-start) | copy-done | bytes 4194328
  2.8 133.1 %shard_map.30 = (f32[3,2,256,256]{3,2,1,0:T(8,128)S(1)}, f32[4,2,3,256,256]{4,3,2,1,0:T(8,128)}, f32[768,768]{1,0:T(8,128)S(1)}) custom-call(f32[2,1,256,8,1,256]{5,4,3,2,1,0:T(1,128)S(1)} %copy-done), custom_call_target="tpu_custom_call" | custom-call | tf_op jit(solution)/shard_map/pallas_call | solution.py:425
  135.9 18.7 %shard_map.31 = (f32[2,1,256,8,1,256]{5,4,3,2,1,0:T(1,128)}, f32[2,1,256,768]{3,2,1,0:T(8,128)}) custom-call(f32[2,1,256,8,1,256]{5,4,3,2,1,0:T(1,128)S(1)} %copy-done, f32[3,2,256,256]{3,2,1,0:T(8,128)S(1)} %get-tuple-element.5.A, f32[4,2,3,256,256]{4,3,2,1,0:T(8,128)} %get-tuple-element.6.B, f32[768,768]{1,0:T(8,128)S(1)} %get-tuple-element.7.V), custom_call_target="tpu_custom_call" | custom-call | tf_op jit(solution)/shard_map/pallas_call | solution.py:499
Async XLA Ops:
  0.6 2.2 %copy-start = (f32[2,1,256,8,1,256]{5,4,3,2,1,0:T(1,128)S(1)}, f32[2,1,256,8,1,256]{5,4,3,2,1,0:T(1,128)}, u32[]{:S(2)}) copy-start(f32[2,1,256,8,1,256]{5,4,3,2,1,0:T(1,128)} %mat.3) | copy-start | bytes 12582916
